TPU v7x, 128 devices: a whole 4x4x4 slice. The times are simulated.
128 devices in a mesh: ctx: 32 (over z_lo, y, x), dp: 4 (over z_hi, core).
Axes of the slice: x: 4, y: 4, z: 4 (z_hi: 2, z_lo: 2; z = z_hi * 2 + z_lo), core: 2. Of those that a mesh axis runs over, the one named last changes fastest.
Arguments:
- tokens: bfloat16 [4, 12288, 4096], P('dp', 'ctx'), may hold values from -6 to 6
- key_input: bfloat16 [4, 12288, 2048], P('dp', 'ctx'), may hold values from -6 to 6
- values: bfloat16 [4, 12288, 2048], P('dp', 'ctx'), may hold values from -6 to 6
- q_weight: bfloat16 [4096, 2048], P(('ctx', 'dp')), may hold values from -0.09375 to 0.09375
- q_spikes: int32 [4, 12288, 2048], P('dp', 'ctx'), may hold values 0 or 1
- k_spikes: int32 [4, 12288, 2048], P('dp', 'ctx'), may hold values 0 or 1
- cotangent: bfloat16 [4, 12288, 2048], P('dp', 'ctx'), may hold values from -6 to 6
Outputs:
- attended: bfloat16 [4, 12288, 2048], P('dp', 'ctx')
- grad_tokens: bfloat16 [4, 12288, 4096], P('dp', 'ctx')
- grad_keys: bfloat16 [4, 12288, 2048], P('dp', 'ctx')
- grad_values: bfloat16 [4, 12288, 2048], P('dp', 'ctx')
All inputs are finite; a program needn't handle non-finite values. No bound on the sum of `q_spikes` or of `k_spikes` on one device may be relied on, other than what follows from the above.
Results may differ from a plain program's by a relative error of at most 0.005.
Values may be sent and summed in bfloat16 or wider, within the bound.
A program may use at most 256 MiB of HBM per device.

v0:
```python
import math

import jax
import jax.numpy as jnp
from jax import lax
from jax.sharding import PartitionSpec as P

HEADS = 16
HEAD = 128


exact_mode = lax.Precision.HIGHEST


def entering(part, axis, combine, identity, reverse):
    count = lax.axis_size(axis)
    place = lax.axis_index(axis)
    ahead = count - 1 - place if reverse else place
    gathered = lax.all_gather(part, axis)
    state = jnp.zeros_like(part) + jnp.asarray(identity, part.dtype)

    def one(lap, state):
        source = count - 1 - lap if reverse else lap
        return combine(state, lax.dynamic_index_in_dim(gathered, source, 0, False))

    return lax.fori_loop(0, ahead, one, state)


def add_states(first_part, second_part):
    return first_part + second_part


def per_device(tokens, key_input, values, q_weight, q_spikes, k_spikes, cotangent):
    batches, length, model_width = tokens.shape
    head_total = q_weight.shape[1]
    sequence = length * lax.axis_size("ctx")
    factor = 3.0 / math.sqrt(HEAD * sequence)
    token_rows = tokens.reshape(batches * length, model_width)
    projected = jnp.dot(
        token_rows,
        lax.all_gather(q_weight, ("ctx", "dp"), axis=0, tiled=True),
        preferred_element_type=jnp.float32,
    )
    queries = (
        projected.reshape(batches, length, head_total) * q_spikes.astype(jnp.float32)
    ).astype(jnp.bfloat16)
    spiked_keys = key_input * k_spikes.astype(jnp.bfloat16)

    def by_heads(array):
        return array.reshape(batches, length, HEADS, HEAD)

    query_wide = by_heads(queries)
    key_wide = by_heads(spiked_keys)
    value_wide = by_heads(values)
    grad_wide = by_heads(cotangent)
    wide_float = jnp.float32
    causal = jnp.tril(jnp.ones((length, length), jnp.float32))
    scores = jnp.einsum("blhe,bmhe->bhlm", query_wide, key_wide, preferred_element_type=wide_float)
    scores = (scores * causal).astype(jnp.bfloat16)
    grad_scores = jnp.einsum(
        "blhf,bmhf->bhlm", grad_wide, value_wide, preferred_element_type=wide_float
    )
    grad_scores = (grad_scores * causal).astype(jnp.bfloat16)
    own_memory = jnp.einsum(
        "blhe,blhf->bhef", key_wide, value_wide, preferred_element_type=wide_float
    )
    own_adjoint = jnp.einsum(
        "blhe,blhf->bhef", query_wide, grad_wide, preferred_element_type=wide_float
    )
    zeroes = jnp.zeros_like(own_memory)
    before = entering(own_memory, "ctx", add_states, zeroes, False)
    later_adjoint = entering(own_adjoint, "ctx", add_states, zeroes, True)
    query_float = query_wide.astype(jnp.float32)
    key_float = key_wide.astype(jnp.float32)
    value_float = value_wide.astype(jnp.float32)
    grad_float = grad_wide.astype(jnp.float32)
    output = jnp.einsum("bhlm,bmhf->blhf", scores, value_wide, preferred_element_type=wide_float)
    output = output + jnp.einsum("blhe,bhef->blhf", query_float, before, precision=exact_mode)
    query_grad = jnp.einsum(
        "bhlm,bmhe->blhe", grad_scores, key_wide, preferred_element_type=wide_float
    )
    query_grad = query_grad + jnp.einsum(
        "blhf,bhef->blhe", grad_float, before, precision=exact_mode
    )
    key_grad = jnp.einsum(
        "bhlm,blhe->bmhe", grad_scores, query_wide, preferred_element_type=wide_float
    )
    key_grad = key_grad + jnp.einsum(
        "bmhf,bhef->bmhe", value_float, later_adjoint, precision=exact_mode
    )
    value_grad = jnp.einsum("bhlm,blhf->bmhf", scores, grad_wide, preferred_element_type=wide_float)
    value_grad = value_grad + jnp.einsum(
        "bmhe,bhef->bmhf", key_float, later_adjoint, precision=exact_mode
    )
    shape_out = (batches, length, head_total)
    attended = (factor * output.reshape(shape_out)).astype(jnp.bfloat16)
    masked_grad = (factor * query_grad.reshape(shape_out) * q_spikes.astype(jnp.float32)).astype(
        jnp.bfloat16
    )
    masked_rows = masked_grad.reshape(batches * length, head_total)
    contract = (((1,), (1,)), ((), ()))
    token_grad = lax.dot_general(
        masked_rows,
        lax.all_gather(q_weight, ("ctx", "dp"), axis=0, tiled=True),
        contract,
        preferred_element_type=jnp.float32,
    )
    grad_tokens = token_grad.reshape(batches, length, model_width).astype(jnp.bfloat16)
    grad_keys = (factor * key_grad.reshape(shape_out) * k_spikes.astype(jnp.float32)).astype(
        jnp.bfloat16
    )
    grad_values = (factor * value_grad.reshape(shape_out)).astype(jnp.bfloat16)
    return (attended, grad_tokens, grad_keys, grad_values)


def solution(mesh):
    in_specs = (
        P("dp", "ctx", None),
        P("dp", "ctx", None),
        P("dp", "ctx", None),
        P(("ctx", "dp"), None),
        P("dp", "ctx", None),
        P("dp", "ctx", None),
        P("dp", "ctx", None),
    )
    out_specs = (
        P("dp", "ctx", None),
        P("dp", "ctx", None),
        P("dp", "ctx", None),
        P("dp", "ctx", None),
    )
    return jax.shard_map(
        per_device, mesh=mesh, in_specs=in_specs, out_specs=out_specs, check_vma=False
    )
```

profile of v0, /device:TPU:0, one launch (start us, length us, event | category | flops | bytes accessed | tf_op | source)
XLA Modules:
  0.0 1036.5 jit_solution(814727491231652069)
XLA Ops:
  8.0 2.7 multiply_bitcast_fusion
  12.3 2.8 copy.38
  20.1 2.6 copy.63
  22.7 203.6 %all-gather.6.cloned.1.call-done = bf16[4096,2048]{1,0:T(8,128)(2,1)} async-done(((bf16[32,2048]{1,0:T(8,128)(2,1)}), bf16[4096,2048]{1,0:T(8,128)(2,1)}) %all-gather.6.cloned.1.call-update) | async-done | bytes 16777232 | tf_op jit(solution)/shard_map/all_gather | solution.py:41
  226.3 12.7 %fusion.5 = bf16[1,384,2048]{2,1,0:T(8,128)(2,1)} fusion(s32[1,384,2048]{2,1,0:T(8,128)} %param.15, bf16[4096,2048]{1,0:T(8,128)(2,1)} %all-gather.6.cloned.1.call-done, bf16[1,384,4096]{2,1,0:T(8,128)(2,1)S(1)} %copy-done), kind=kOutput, calls=%fused_computation.13 | convolution fusion | flops 6444810240 | bytes 24641536 | tf_op jit(solution)/shard_map/dot_general | solution.py:39
  240.9 3.4 fusion.28
  244.3 5.7 multiply_convert_fusion
  250.1 4.2 multiply_convert_fusion.1
  254.3 337.6 %all-gather.8.cloned.1.call-done = f32[512,128,128]{2,1,0:T(8,128)} async-done(((f32[16,128,128]{2,1,0:T(8,128)}), f32[512,128,128]{2,1,0:T(8,128)}) %all-gather.8.cloned.1.call-update) | async-done | bytes 33554448 | tf_op jit(solution)/shard_map/all_gather | solution.py:19
  594.6 4.2 fusion.4
  598.8 2.7 copy.57
  601.5 3.0 fusion.18
  604.5 5.7 add_multiply_fusion.1
  610.2 3.6 copy.61
  613.8 13.4 %fusion = bf16[1,384,4096]{2,1,0:T(8,128)(2,1)} fusion(bf16[4096,2048]{1,0:T(8,128)(2,1)} %all-gather.6.cloned.1.call-done, f32[1,384,2048]{2,1,0:T(8,128)} %copy.61, s32[1,384,2048]{2,1,0:T(8,128)} %param.15), kind=kOutput, calls=%fused_computation.5 | convolution fusion | flops 6446383104 | bytes 26214400 | tf_op jit(solution)/shard_map/dot_general | solution.py:102
  627.2 327.7 %all-gather.10.cloned.1.call-done = f32[512,128,128]{2,1,0:T(8,128)} async-done(((f32[16,128,128]{2,1,0:T(8,128)}), f32[512,128,128]{2,1,0:T(8,128)}) %all-gather.10.cloned.1.call-update) | async-done | bytes 33554448 | tf_op jit(solution)/shard_map/all_gather | solution.py:19
  955.0 47.1 %while.23 = (s32[]{:T(128)}, f32[1,16,128,128]{3,2,1,0:T(8,128)S(1)}, s32[]{:T(128)}, f32[32,1,16,128,128]{4,3,2,1,0:T(8,128)}, s32[]{:T(128)}, /*index=5*/s32[]{:T(128)}, s32[]{:T(128)}, s32[]{:T(128)}) while((s32[]{:T(128)}, f32[1,16,128,128]{3,2,1,0:T(8,128)S(1)}, s32[]{:T(128)}, f32[32,1,16,128,128]{4,3,2,1,0:T(8,128)}, s32[]{:T(128)}, ...), condition=%wide.region_3.4_spmd, body=%wide.region_2.3_spmd.sunk | while | flops 262150 | bytes 3145871 | solution.py:26
  1002.1 3.6 fusion.16
  1005.8 3.7 fusion.12
  1009.5 5.3 add_multiply_fusion
  1014.8 3.8 copy.53
  1018.6 3.9 multiply_convert_fusion.2
  1022.5 4.9 fusion.2
  1027.4 2.6 copy.58
  (70 shorter events, 58.1 us)
Async XLA Ops:
  7.2 219.2 %copy-start = (bf16[1,384,4096]{2,1,0:T(8,128)(2,1)S(1)}, bf16[1,384,4096]{2,1,0:T(8,128)(2,1)}, u32[]{:S(2)}) copy-start(bf16[1,384,4096]{2,1,0:T(8,128)(2,1)} %param.11) | copy-start | bytes 9437188
  7.2 219.1 %all-gather.6.cloned.1.call-start = ((), (), s32[]{:S(2)}) async-start(), calls=%async_computation | async-start | bytes 16908288 | tf_op jit(solution)/shard_map/all_gather | solution.py:41
  7.9 584.0 %all-gather.8.cloned.1.call-start = ((), (), s32[]{:S(2)}) async-start(), calls=%async_computation.1 | async-start | bytes 34603008 | tf_op jit(solution)/shard_map/all_gather | solution.py:19
  15.1 3.1 copy-start.8
  17.0 1.2 copy-start.3
  20.0 934.9 %all-gather.10.cloned.1.call-start = ((), (), s32[]{:S(2)}) async-start(), calls=%async_computation.2 | async-start | bytes 34603008 | tf_op jit(solution)/shard_map/all_gather | solution.py:19
  240.9 3.5 copy-start.4
  244.3 5.8 copy-start.6
  592.2 2.3 copy-start.2
  601.5 3.0 copy-start.9
  1002.1 3.6 copy-start.7
  1014.8 3.8 copy-start.10
  1018.6 3.9 copy-start.5
  1018.6 3.9 copy-start.11
  1022.5 7.5 copy-start.1
Sparse Core Ops, SparseCore 0:
  9.7 216.5 all-gather.5
  228.5 363.3 all-gather.7
  593.6 361.3 all-gather.9
where the time goes:
time: 1040 us
  waiting for transfers between devices  870 us (84%)
  matrix products  73 us (7%)
  other arithmetic  52.8 us (5%)
  local copies, waits for them, and re-layouts  25.8 us (2%)
  between operations  13.9 us (1%)
    all_gather x2, waiting for transfers between devices, entering(): gathered = lax.all_gather(part, axis)  665 us
    all_gather x1, waiting for transfers between devices, per_device(): lax.all_gather(q_weight, ('ctx', 'dp'), axis=0, tiled=True)  204 us
    add x31, other arithmetic, add_states(): return first_part + second_part  46.2 us
  transfers between devices with their start and end apart: 3, of which 3 were waited for; matrix products, arithmetic and copies ran while one was open for 7% of the time, Pallas kernels for 0%

commit v1 on v0

v1 whole, which is shorter than its diff:
```python
import functools
import math

import jax
import jax.numpy as jnp
from jax import lax
from jax.experimental import pallas as pl
from jax.experimental.pallas import tpu as pltpu
from jax.sharding import PartitionSpec as P

HEADS = 16
HEAD = 128
GROUPS = 8
GCOLS = 256
N_CTX = 32
PIECE = HEADS * HEAD // N_CTX
MESH = pl.DeviceIdType.MESH
ORDERS = ((0, 1, 2), (1, 2, 0), (2, 0, 1))


def place():
    ctx = lax.axis_index("ctx")
    dp = lax.axis_index("dp")
    x = lax.rem(ctx, 4)
    y = lax.rem(ctx // 4, 4)
    z = (dp // 2) * 2 + ctx // 16
    return (x, y, z), lax.rem(dp, 2)


def device_of(at, core):
    x, y, z = at
    return (lax.rem(z, 2) * 16 + y * 4 + x, (z // 2) * 2 + core)


def moved(at, axis, by):
    out = list(at)
    out[axis] = lax.rem(out[axis] + by, 4)
    return tuple(out)


def view(buf, group, at, core, whole):
    def pick(axis):
        return slice(None) if axis in whole else None

    x, y, z = at
    sx = slice(None) if 0 in whole else x
    sy = slice(None) if 1 in whole else y
    slo = slice(None) if 2 in whole else lax.rem(z, 2)
    shi = slice(None) if 2 in whole else z // 2
    return buf.at[group, slo, sy, sx, shi, core]


def gather_kernel(w_ref, out_ref, own_sem, send_sem, recv_sem, sib_sems):
    at, core = place()
    buf = out_ref
    barrier = pltpu.get_barrier_semaphore()
    for axis in range(3):
        for by in (1, 2, 3):
            pl.semaphore_signal(
                barrier, 1, device_id=device_of(moved(at, axis, by), core), device_id_type=MESH
            )
    pl.semaphore_signal(barrier, 1, device_id=device_of(at, 1 - core), device_id_type=MESH)
    own = []
    for g in range(GROUPS):
        copy = pltpu.make_async_copy(
            w_ref.at[:, pl.ds(g * GCOLS, GCOLS)], view(buf, g, at, core, ()), own_sem.at[g]
        )
        copy.start()
        own.append(copy)
    pl.semaphore_wait(barrier, 10)

    def phase(g, number):
        order = ORDERS[g % 3]
        whole = order[:number]
        part = view(buf, g, at, core, whole)
        copies = []
        for by in (1, 3, 2):
            copy = pltpu.make_async_remote_copy(
                src_ref=part,
                dst_ref=part,
                send_sem=send_sem.at[g, number, by - 1],
                recv_sem=recv_sem.at[g, number, by - 1],
                device_id=device_of(moved(at, order[number], by), core),
                device_id_type=MESH,
            )
            copy.start()
            copies.append(copy)
        return copies

    def sibling(g):
        part = view(buf, g, at, core, (0, 1, 2))
        copy = pltpu.make_async_remote_copy(
            src_ref=part,
            dst_ref=part,
            send_sem=sib_sems.at[0, g],
            recv_sem=sib_sems.at[1, g],
            device_id=device_of(at, 1 - core),
            device_id_type=MESH,
        )
        copy.start()
        return copy

    flights = {}
    for step in range(GROUPS + 3):
        if step < GROUPS:
            own[step].wait()
            flights[step, 0] = phase(step, 0)
        for number in (1, 2, 3):
            g = step - number
            if 0 <= g < GROUPS:
                for copy in flights[g, number - 1]:
                    copy.wait_recv()
                if number < 3:
                    flights[g, number] = phase(g, number)
                else:
                    flights[g, 3] = [sibling(g)]
    for g in range(GROUPS):
        for number in range(3):
            for copy in flights[g, number]:
                copy.wait_send()
        flights[g, 3][0].wait()


def gather(weight):
    rows, columns = weight.shape
    out = pl.pallas_call(
        gather_kernel,
        out_shape=jax.ShapeDtypeStruct((GROUPS, 2, 4, 4, 2, 2, rows, GCOLS), weight.dtype),
        in_specs=[pl.BlockSpec(memory_space=pl.ANY)],
        out_specs=pl.BlockSpec(memory_space=pl.ANY),
        scratch_shapes=[
            pltpu.SemaphoreType.DMA((GROUPS,)),
            pltpu.SemaphoreType.DMA((GROUPS, 3, 3)),
            pltpu.SemaphoreType.DMA((GROUPS, 3, 3)),
            pltpu.SemaphoreType.DMA((2, GROUPS)),
        ],
        compiler_params=pltpu.CompilerParams(collective_id=0, has_side_effects=True),
    )(weight)
    return out.reshape(GROUPS, rows * 128, GCOLS)


def scan_kernel(reverse, part_ref, out_ref, inbox, outbox, send_sem, recv_sem):
    me = lax.axis_index("ctx")
    dp = lax.axis_index("dp")
    barrier = pltpu.get_barrier_semaphore()

    def greet(step, carry):
        pl.semaphore_signal(
            barrier, 1, device_id=(lax.rem(me + step, N_CTX), dp), device_id_type=MESH
        )
        return carry

    lax.fori_loop(1, N_CTX, greet, 0)
    pl.semaphore_wait(barrier, N_CTX - 1)

    def exchange(src, dst, number):
        def send(step, carry):
            other = lax.rem(me + step, N_CTX)
            pltpu.make_async_remote_copy(
                src_ref=src.at[other],
                dst_ref=dst.at[me],
                send_sem=send_sem.at[number],
                recv_sem=recv_sem.at[number],
                device_id=(other, dp),
                device_id_type=MESH,
            ).start()
            return carry

        lax.fori_loop(1, N_CTX, send, 0)
        dst[pl.ds(me, 1)] = src[pl.ds(me, 1)]
        most = pl.ds(0, N_CTX - 1)
        pltpu.make_async_copy(src.at[most], dst.at[most], recv_sem.at[number]).wait()
        pltpu.make_async_copy(src.at[most], dst.at[most], send_sem.at[number]).wait()

    exchange(part_ref, inbox, 0)

    def add(step, total):
        source = N_CTX - 1 - step if reverse else step
        outbox[source] = total.astype(outbox.dtype)
        return total + inbox[source].astype(jnp.float32)

    lax.fori_loop(0, N_CTX, add, jnp.zeros(inbox.shape[1:], jnp.float32))
    exchange(outbox, out_ref, 1)


def entering(part, reverse, number):
    pieces = part.astype(jnp.bfloat16).reshape(N_CTX, PIECE, HEAD)
    out = pl.pallas_call(
        functools.partial(scan_kernel, reverse),
        out_shape=jax.ShapeDtypeStruct(pieces.shape, pieces.dtype),
        in_specs=[pl.BlockSpec(memory_space=pltpu.VMEM)],
        out_specs=pl.BlockSpec(memory_space=pltpu.VMEM),
        scratch_shapes=[
            pltpu.VMEM(pieces.shape, pieces.dtype),
            pltpu.VMEM(pieces.shape, pieces.dtype),
            pltpu.SemaphoreType.DMA((2,)),
            pltpu.SemaphoreType.DMA((2,)),
        ],
        compiler_params=pltpu.CompilerParams(collective_id=number, has_side_effects=True),
    )(pieces)
    return out.reshape(part.shape)


def per_device(tokens, key_input, values, q_weight, q_spikes, k_spikes, cotangent):
    batches, length, model_width = tokens.shape
    head_total = q_weight.shape[1]
    sequence = length * lax.axis_size("ctx")
    factor = 3.0 / math.sqrt(HEAD * sequence)
    wide_float = jnp.float32
    token_rows = tokens.reshape(batches * length, model_width)
    spiked_keys = key_input * k_spikes.astype(jnp.bfloat16)

    def by_heads(array):
        return array.reshape(batches, length, HEADS, HEAD)

    key_wide = by_heads(spiked_keys)
    value_wide = by_heads(values)
    grad_wide = by_heads(cotangent)
    own_memory = jnp.einsum(
        "blhe,blhf->bhef", key_wide, value_wide, preferred_element_type=wide_float
    )
    before = entering(own_memory, False, 1)
    weight = gather(q_weight)
    projected = jnp.einsum("td,gdf->tgf", token_rows, weight, preferred_element_type=jnp.float32)
    queries = (
        projected.reshape(batches, length, head_total) * q_spikes.astype(jnp.float32)
    ).astype(jnp.bfloat16)
    query_wide = by_heads(queries)
    own_adjoint = jnp.einsum(
        "blhe,blhf->bhef", query_wide, grad_wide, preferred_element_type=wide_float
    )
    later_adjoint = entering(own_adjoint, True, 2)
    causal = jnp.tril(jnp.ones((length, length), jnp.float32))
    scores = jnp.einsum("blhe,bmhe->bhlm", query_wide, key_wide, preferred_element_type=wide_float)
    scores = (scores * causal).astype(jnp.bfloat16)
    grad_scores = jnp.einsum(
        "blhf,bmhf->bhlm", grad_wide, value_wide, preferred_element_type=wide_float
    )
    grad_scores = (grad_scores * causal).astype(jnp.bfloat16)
    output = jnp.einsum("bhlm,bmhf->blhf", scores, value_wide, preferred_element_type=wide_float)
    output = output + jnp.einsum(
        "blhe,bhef->blhf", query_wide, before, preferred_element_type=wide_float
    )
    query_grad = jnp.einsum(
        "bhlm,bmhe->blhe", grad_scores, key_wide, preferred_element_type=wide_float
    )
    query_grad = query_grad + jnp.einsum(
        "blhf,bhef->blhe", grad_wide, before, preferred_element_type=wide_float
    )
    key_grad = jnp.einsum(
        "bhlm,blhe->bmhe", grad_scores, query_wide, preferred_element_type=wide_float
    )
    key_grad = key_grad + jnp.einsum(
        "bmhf,bhef->bmhe", value_wide, later_adjoint, preferred_element_type=wide_float
    )
    value_grad = jnp.einsum("bhlm,blhf->bmhf", scores, grad_wide, preferred_element_type=wide_float)
    value_grad = value_grad + jnp.einsum(
        "bmhe,bhef->bmhf", key_wide, later_adjoint, preferred_element_type=wide_float
    )
    shape_out = (batches, length, head_total)
    attended = (factor * output.reshape(shape_out)).astype(jnp.bfloat16)
    masked_grad = (factor * query_grad.reshape(shape_out) * q_spikes.astype(jnp.float32)).astype(
        jnp.bfloat16
    )
    masked_rows = masked_grad.reshape(batches * length, GROUPS, GCOLS)
    token_grad = jnp.einsum("tgf,gdf->td", masked_rows, weight, preferred_element_type=jnp.float32)
    grad_tokens = token_grad.reshape(batches, length, model_width).astype(jnp.bfloat16)
    grad_keys = (factor * key_grad.reshape(shape_out) * k_spikes.astype(jnp.float32)).astype(
        jnp.bfloat16
    )
    grad_values = (factor * value_grad.reshape(shape_out)).astype(jnp.bfloat16)
    return (attended, grad_tokens, grad_keys, grad_values)


def solution(mesh):
    rows = P("dp", "ctx", None)
    in_specs = (rows, rows, rows, P(("ctx", "dp"), None), rows, rows, rows)
    return jax.shard_map(
        per_device, mesh=mesh, in_specs=in_specs, out_specs=(rows,) * 4, check_vma=False
    )
```

time: 1040 us -> 233 us (0.22)
  waiting for transfers between devices: 870 us -> 0 us
  Pallas kernels: 0 us -> 121 us
  other arithmetic: 52.8 us -> 11.1 us
  matrix products: 73 us -> 53.2 us
  local copies, waits for them, and re-layouts: 25.8 us -> 45.2 us
  between operations: 13.9 us -> 0.87 us
    all_gather x3 -> x0, waiting for transfers between devices: 869 us -> none  [the longest x2 665 us: entering(): gathered = lax.all_gather(part, axis)]
    pallas_call x0 -> x3, Pallas kernels: none -> 121 us  [the longest x1 72.8 us: gather(): pl.pallas_call(gather_kernel, out_shape=jax.ShapeDtypeStruct((GROUPS, 2,...]
    add x31 -> x0, other arithmetic: 46.2 us -> none  [add_states(): return first_part + second_part]
    reshape x1 -> x2, local copies, waits for them, and re-layouts: 1.87 us -> 22.7 us  [the longest x1 20.9 us: gather(): return out.reshape(GROUPS, rows * 128, GCOLS)]
  transfers between devices with their start and end apart: 3 -> 0, of which waited for: 3 -> 0; matrix products, arithmetic and copies ran while one was open for 7% -> 0% of each run, Pallas kernels for 0% -> 0%
where the time goes in v1:
time: 233 us; the launch traced here: 232 us
  Pallas kernels  121 us (52%)
  matrix products  53.2 us (23%)
  local copies, waits for them, and re-layouts  45.2 us (19%)
  other arithmetic  11.1 us (5%)
    pallas_call x1, Pallas kernels, gather(): pl.pallas_call(gather_kernel, out_shape=jax.ShapeDtypeStruct((GROUPS, 2,...  72.8 us
    pallas_call x2, Pallas kernels, entering(): pl.pallas_call(functools.partial(scan_kernel, reverse), out_shape=jax.Sha...  48.5 us
    reshape x1, local copies, waits for them, and re-layouts, gather(): return out.reshape(GROUPS, rows * 128, GCOLS)  20.9 us
    dot_general x1, matrix products, per_device(): jnp.einsum('td,gdf->tgf', token_rows, weight, preferred_element_type=jnp....  12.7 us
    dot_general x1, matrix products, per_device(): jnp.einsum('tgf,gdf->td', masked_rows, weight, preferred_element_type=jnp...  11.7 us
    unnamed x39, local copies, waits for them, and re-layouts  11.6 us
    another operation x2, local copies, waits for them, and re-layouts  4.89 us
    dot_general x1, matrix products, per_device(): jnp.einsum('bhlm,blhf->bmhf', scores, grad_wide, preferred_element_type=w...  4.88 us

profile of v1, /device:TPU:0, one launch (start us, length us, event | category | flops | bytes accessed | tf_op | source)
XLA Modules:
  0.0 231.8 jit_solution(18115456232451202505)
XLA Ops:
  0.6 2.7 %multiply_bitcast_fusion = bf16[48,8,16,128]{3,1,2,0:T(8,128)(2,1)S(1)} fusion(bf16[1,384,2048]{2,1,0:T(8,128)(2,1)} %param.8, s32[1,384,2048]{2,1,0:T(8,128)} %param.12), kind=kLoop, calls=%fused_computation.19 | loop fusion | flops 1572864 | bytes 6291456
  4.9 2.8 %copy.38 = bf16[384,16,128]{0,2,1:T(8,128)(2,1)} copy(bf16[384,16,128]{2,1,0:T(8,128)(2,1)} %bitcast.99) | data formatting | bytes 3145728 | tf_op jit(solution)/shard_map/reshape.1
  7.8 1.9 copy.64
  12.5 25.3 %shard_map.103 = bf16[32,64,128]{2,1,0:T(8,128)(2,1)} custom-call(bf16[32,64,128]{2,1,0:T(8,128)(2,1)} %bitcast.119), custom_call_target="tpu_custom_call" | custom-call | tf_op jit(solution)/shard_map/pallas_call | solution.py:188
  37.8 72.8 %shard_map.102 = bf16[8,2,4,4,2,2,32,256]{7,6,5,4,3,2,1,0:T(8,128)(2,1)} custom-call(bf16[32,2048]{1,0:T(8,128)(2,1)} %w_ref.1), custom_call_target="tpu_custom_call" | custom-call | tf_op jit(solution)/shard_map/pallas_call | solution.py:126
  110.6 20.9 %copy.34 = bf16[8,4096,256]{1,2,0:T(8,128)(2,1)} copy(bf16[8,4096,256]{2,1,0:T(8,128)(2,1)} %bitcast.87) | data formatting | bytes 33554432 | tf_op jit(solution)/shard_map/reshape | solution.py:139
  131.5 12.7 %fusion.5 = bf16[1,384,2048]{2,1,0:T(8,128)(2,1)} fusion(s32[1,384,2048]{2,1,0:T(8,128)} %param.11, bf16[2048,4096]{1,0:T(8,128)(2,1)} %bitcast.106, bf16[1,384,4096]{2,1,0:T(8,128)(2,1)S(1)} %copy-done), kind=kOutput, calls=%fused_computation.11 | convolution fusion | flops 6444810240 | bytes 24641536 | tf_op jit(solution)/shard_map/td,gdf->tgf/dot_general | solution.py:224
  144.2 1.9 copy.61
  146.1 1.8 fusion.19
  148.8 2.0 multiply_convert_fusion.1
  150.8 1.7 fusion.4
  154.6 2.0 copy.62
  156.6 4.0 %multiply_convert_fusion = bf16[16,384,384]{2,1,0:T(8,128)(2,1)S(1)} fusion(f32[384,384]{1,0:T(8,128)} %copy-done.12, bf16[384,16,128]{0,2,1:T(8,128)(2,1)S(1)} %bitcast.95, bf16[384,16,128]{2,1,0:T(8,128)(2,1)} %bitcast.103), kind=kOutput, calls=%fused_computation | convolution fusion | flops 608698368 | bytes 8454144 | tf_op jit(solution)/shard_map/blhf,bmhf->bhlm/dot_general | solution.py:236
  162.8 2.3 add_multiply_fusion.1
  165.1 3.6 %copy.60 = f32[1,384,2048]{2,1,0:T(8,128)} copy(f32[1,384,2048]{1,2,0:T(8,128)} %bitcast.107) | data formatting | bytes 6291456 | tf_op jit(solution)/shard_map/mul | solution.py:262
  168.7 3.5 %multiply_convert_fusion.3 = bf16[1,384,2048]{2,1,0:T(8,128)(2,1)S(1)} fusion(f32[1,384,2048]{2,1,0:T(8,128)} %copy.60, s32[1,384,2048]{2,1,0:T(8,128)} %param.11), kind=kLoop, calls=%fused_computation.16 | loop fusion | flops 2359296 | bytes 7864320 | tf_op jit(solution)/shard_map/convert_element_type | solution.py:262
  172.8 11.7 %fusion = bf16[1,384,4096]{2,1,0:T(8,128)(2,1)} fusion(bf16[8,4096,256]{2,1,0:T(8,128)(2,1)} %bitcast.88, bf16[384,8,256]{2,1,0:T(8,128)(2,1)S(1)} %bitcast.118), kind=kOutput, calls=%fused_computation.3 | convolution fusion | flops 6444023808 | bytes 21495808 | tf_op jit(solution)/shard_map/tgf,gdf->td/dot_general | solution.py:266
  184.5 2.9 %fusion.21 = f32[16,128,384]{2,1,0:T(8,128)} fusion(bf16[384,16,128]{0,2,1:T(8,128)(2,1)S(1)} %bitcast.93, bf16[16,384,384]{2,1,0:T(8,128)(2,1)S(1)} %bitcast.90), kind=kOutput, calls=%fused_computation.33 | convolution fusion | flops 603979776 | bytes 9437184 | tf_op jit(solution)/shard_map/bhlm,blhe->bmhe/dot_general | solution.py:250
  188.9 23.3 %shard_map.104 = bf16[32,64,128]{2,1,0:T(8,128)(2,1)} custom-call(bf16[32,64,128]{2,1,0:T(8,128)(2,1)} %bitcast.116), custom_call_target="tpu_custom_call" | custom-call | tf_op jit(solution)/shard_map/pallas_call | solution.py:188
  212.2 3.5 %add_multiply_fusion = f32[16,128,384]{2,1,0:T(8,128)S(1)} fusion(f32[16,128,384]{2,1,0:T(8,128)} %fusion.21, bf16[16,128,128]{2,1,0:T(8,128)(2,1)} %bitcast.114, bf16[384,16,128]{2,1,0:T(8,128)(2,1)} %bitcast.104), kind=kOutput, calls=%fused_computation.15 | convolution fusion | flops 202899456 | bytes 8388608 | tf_op jit(solution)/shard_map/bmhf,bhef->bmhe/dot_general | solution.py:253
  215.7 2.4 %copy.52 = f32[1,384,2048]{2,1,0:T(8,128)} copy(f32[1,384,2048]{1,2,0:T(8,128)S(1)} %bitcast.108) | data formatting | bytes 6291456 | tf_op jit(solution)/shard_map/mul | solution.py:268
  218.1 4.8 %multiply_convert_fusion.2 = bf16[1,384,2048]{2,1,0:T(8,128)(2,1)} fusion(f32[1,384,2048]{2,1,0:T(8,128)} %copy.52, s32[1,384,2048]{2,1,0:T(8,128)} %param.12), kind=kLoop, calls=%fused_computation.14 | loop fusion | flops 2359296 | bytes 7864320 | tf_op jit(solution)/shard_map/convert_element_type | solution.py:268
  224.3 4.9 %fusion.2 = bf16[16,128,384]{2,1,0:T(8,128)(2,1)} fusion(f32[16,128,384]{2,1,0:T(8,128)S(1)} %fusion.11, bf16[384,16,128]{0,2,1:T(8,128)(2,1)S(1)} %bitcast.98, bf16[16,384,384]{2,1,0:T(8,128)(2,1)} %copy-done.3), kind=kOutput, calls=%fused_computation.6 | convolution fusion | flops 606339072 | bytes 11010048 | tf_op jit(solution)/shard_map/bhlm,blhf->bmhf/dot_general | solution.py:256
  229.2 2.6 %copy.57 = bf16[1,384,2048]{2,1,0:T(8,128)(2,1)} copy(bf16[1,384,2048]{1,2,0:T(8,128)(2,1)} %bitcast.109) | data formatting | bytes 3145728
  (43 shorter events, 12.8 us)
Async XLA Ops:
  0.6 130.9 %copy-start = (bf16[1,384,4096]{2,1,0:T(8,128)(2,1)S(1)}, bf16[1,384,4096]{2,1,0:T(8,128)(2,1)}, u32[]{:S(2)}) copy-start(bf16[1,384,4096]{2,1,0:T(8,128)(2,1)} %param.7) | copy-start | bytes 9437188
  7.8 3.1 %copy-start.10 = (bf16[384,16,128]{0,2,1:T(8,128)(2,1)S(1)}, bf16[384,16,128]{0,2,1:T(8,128)(2,1)}, u32[]{:S(2)}) copy-start(bf16[384,16,128]{0,2,1:T(8,128)(2,1)} %copy.38) | copy-start | bytes 4718596
  9.7 1.1 copy-start.8
  146.1 2.7 %copy-start.6 = (bf16[48,8,16,128]{3,2,1,0:T(8,128)(2,1)S(1)}, bf16[48,8,16,128]{3,2,1,0:T(8,128)(2,1)}, u32[]{:S(2)}) copy-start(bf16[48,8,16,128]{3,2,1,0:T(8,128)(2,1)} %copy.63) | copy-start | bytes 4718596
  147.9 0.8 copy-start.12
  148.8 2.1 copy-start.9
  150.8 2.1 copy-start.3
  156.6 30.7 %copy-start.4 = (bf16[1,384,2048]{1,2,0:T(8,128)(2,1)}, bf16[1,384,2048]{1,2,0:T(8,128)(2,1)S(1)}, u32[]{:S(2)}) copy-start(bf16[1,384,2048]{1,2,0:T(8,128)(2,1)S(1)} %copy.62) | copy-start | bytes 4718596
  156.6 4.0 %copy-start.11 = (bf16[384,16,128]{0,2,1:T(8,128)(2,1)S(1)}, bf16[384,16,128]{0,2,1:T(8,128)(2,1)}, u32[]{:S(2)}) copy-start(bf16[384,16,128]{0,2,1:T(8,128)(2,1)} %copy.38) | copy-start | bytes 4718596
  160.6 2.2 copy-start.2
  160.6 2.2 copy-start.13
  172.2 12.2 %slice-start = ((s8[4718592]{0:T(1024)(128)(4,1)}), s8[4194304]{0:T(1024)(128)(4,1)S(1)}, s32[]{:S(2)}) async-start(s8[4718592]{0:T(1024)(128)(4,1)} %bitcast.89), calls=%async_computation | async-start | bytes 8388608
  172.7 11.7 %slice-start.1 = ((s8[4718592]{0:T(1024)(128)(4,1)}), s8[524288]{0:T(1024)(128)(4,1)S(1)}, s32[]{:S(2)}) async-start(s8[4718592]{0:T(1024)(128)(4,1)} %bitcast.89), calls=%async_computation.1 | async-start | bytes 1048576
  218.1 4.8 %copy-start.7 = (bf16[48,8,16,128]{3,2,1,0:T(8,128)(2,1)S(1)}, bf16[48,8,16,128]{3,2,1,0:T(8,128)(2,1)}, u32[]{:S(2)}) copy-start(bf16[48,8,16,128]{3,2,1,0:T(8,128)(2,1)} %copy.63) | copy-start | bytes 4718596
  218.1 4.8 %copy-start.14 = (bf16[32,64,128]{2,1,0:T(8,128)(2,1)S(1)}, bf16[32,64,128]{2,1,0:T(8,128)(2,1)}, u32[]{:S(2)}) copy-start(bf16[32,64,128]{2,1,0:T(8,128)(2,1)} %shard_map.104) | copy-start | bytes 1572868
  222.9 1.4 copy-start.5
  224.3 7.5 %copy-start.1 = (bf16[1,384,4096]{2,1,0:T(8,128)(2,1)S(1)}, bf16[1,384,4096]{2,1,0:T(8,128)(2,1)}, u32[]{:S(2)}) copy-start(bf16[1,384,4096]{2,1,0:T(8,128)(2,1)} %param.7) | copy-start | bytes 9437188

commit v2 on v0

v2 whole, which is shorter than its diff:
```python
import functools
import math

import jax
import jax.numpy as jnp
from jax import lax
from jax.experimental import pallas as pl
from jax.experimental.pallas import tpu as pltpu
from jax.sharding import PartitionSpec as P

HEADS = 16
HEAD = 128
TOK = 384
D = 4096
HD = HEADS * HEAD
GROUPS = 8
GCOLS = 256
N_CTX = 32
ROWS = 32
FIRST = 12
MESH = pl.DeviceIdType.MESH
ORDERS = ((0, 1, 2), (1, 2, 0), (2, 0, 1))
BF16 = jnp.bfloat16
F32 = jnp.float32
NT = (((1,), (1,)), ((), ()))
TN = (((0,), (0,)), ((), ()))


def place():
    ctx = lax.axis_index("ctx")
    dp = lax.axis_index("dp")
    x = lax.rem(ctx, 4)
    y = lax.rem(ctx // 4, 4)
    z = (dp // 2) * 2 + ctx // 16
    return (x, y, z), lax.rem(dp, 2)


def device_of(at, core):
    x, y, z = at
    return (lax.rem(z, 2) * 16 + y * 4 + x, (z // 2) * 2 + core)


def moved(at, axis, by):
    out = list(at)
    out[axis] = lax.rem(out[axis] + by, 4)
    return tuple(out)


def view(buf, group, at, core, whole, half=None):
    picks = []
    for axis in range(2):
        if half is not None and half[0] == axis:
            picks.append(pl.ds(2 * half[1], 2))
        elif axis in whole:
            picks.append(slice(None))
        else:
            picks.append(at[axis])
    low = slice(None) if 2 in whole else lax.rem(at[2], 2)
    high = slice(None) if 2 in whole else at[2] // 2
    return buf.at[group, low, picks[1], picks[0], high, core]


def dot(a, b, dims=(((1,), (0,)), ((), ()))):
    return lax.dot_general(a, b, dims, preferred_element_type=F32)


def layer_kernel(
    factor,
    tok_hbm,
    key_hbm,
    val_hbm,
    w_hbm,
    qsp_hbm,
    ksp_hbm,
    cot_hbm,
    att_hbm,
    gtok_hbm,
    gkey_hbm,
    gval_hbm,
    wbuf,
    tok,
    keys,
    val,
    cot,
    qsp,
    ksp,
    mg,
    kgrad,
    vgrad,
    att,
    gtok,
    gkey,
    gval,
    m_send,
    m_in,
    m_out,
    m_state,
    a_send,
    a_in,
    a_out,
    a_state,
    b_send,
    b_in,
    b_out,
    b_state,
    own_sem,
    load_sem,
    send_sem,
    recv_sem,
    sib_sem,
    scan_sem,
    store_sem,
):
    at, core = place()
    ctx = lax.axis_index("ctx")
    dp = lax.axis_index("dp")
    other_core = device_of(at, 1 - core)

    own = []
    for g in range(GROUPS):
        copy = pltpu.make_async_copy(
            w_hbm.at[:, pl.ds(g * GCOLS, GCOLS)], view(wbuf, g, at, core, ()), own_sem.at[g]
        )
        copy.start()
        own.append(copy)

    loads = []
    for number, (src, dst) in enumerate(
        (
            (key_hbm, keys),
            (ksp_hbm, ksp),
            (val_hbm, val),
            (cot_hbm, cot),
            (tok_hbm, tok),
            (qsp_hbm, qsp),
        )
    ):
        copy = pltpu.make_async_copy(src, dst, load_sem.at[number])
        copy.start()
        loads.append(copy)

    barrier = pltpu.get_barrier_semaphore()

    def greet(step, carry):
        pl.semaphore_signal(
            barrier, 1, device_id=(lax.rem(ctx + step, N_CTX), dp), device_id_type=MESH
        )
        return carry

    lax.fori_loop(1, N_CTX, greet, 0)
    far_z = 1 - at[2] // 2
    for low in (0, 1):
        pl.semaphore_signal(
            barrier,
            1,
            device_id=(low * 16 + at[1] * 4 + at[0], far_z * 2 + core),
            device_id_type=MESH,
        )
    pl.semaphore_signal(barrier, 1, device_id=other_core, device_id_type=MESH)
    pl.semaphore_wait(barrier, N_CTX + 2)

    ended = []

    def send(part, g, slot, target):
        copy = pltpu.make_async_remote_copy(
            src_ref=part,
            dst_ref=part,
            send_sem=send_sem.at[g, slot],
            recv_sem=recv_sem.at[g, slot],
            device_id=target,
            device_id_type=MESH,
        )
        copy.start()
        ended.append(copy)
        return copy

    def spread(g, number):
        order = ORDERS[g % 3]
        part = view(wbuf, g, at, core, order[:number])
        return [
            send(part, g, 3 * number + by - 1, device_of(moved(at, order[number], by), core))
            for by in (1, 3, 2)
        ]

    def to_sibling(g, slot, where):
        part = view(wbuf, g, where, core, ORDERS[g % 3][:2])
        copy = pltpu.make_async_remote_copy(
            src_ref=part,
            dst_ref=part,
            send_sem=sib_sem.at[0, g, slot],
            recv_sem=sib_sem.at[1, g, slot],
            device_id=other_core,
            device_id_type=MESH,
        )
        copy.start()
        ended.append(copy)
        return copy

    flights = {}

    def first(g):
        own[g].wait()
        flights[g, 0] = spread(g, 0)

    def second(g):
        for copy in flights[g, 0]:
            copy.wait_recv()
        flights[g, 1] = spread(g, 1)

    def third(g):
        for copy in flights[g, 1]:
            copy.wait_recv()
        order = ORDERS[g % 3]
        part = view(wbuf, g, at, core, order[:2])
        flights[g, 2] = [
            send(part, g, 6, device_of(moved(at, order[2], 1), core)),
            send(part, g, 7, device_of(moved(at, order[2], 3), core)),
        ]
        flights[g, 4] = [to_sibling(g, 0, at)]

    def fourth(g):
        order = ORDERS[g % 3]
        left, right = moved(at, order[2], 3), moved(at, order[2], 1)
        split = 0 if order[2] == 1 else 1
        flights[g, 2][0].wait_recv()
        one = send(
            view(wbuf, g, left, core, order[:2], (split, 0)), g, 8, device_of(right, core)
        )
        flights[g, 4].append(to_sibling(g, 1, left))
        flights[g, 2][1].wait_recv()
        two = send(
            view(wbuf, g, right, core, order[:2], (split, 1)), g, 9, device_of(left, core)
        )
        flights[g, 4].append(to_sibling(g, 2, right))
        flights[g, 3] = [one, two]

    def fifth(g):
        for copy in flights[g, 3]:
            copy.wait_recv()
        flights[g, 4].append(to_sibling(g, 3, moved(at, ORDERS[g % 3][2], 2)))

    def arrived(g):
        for copy in flights[g, 4]:
            copy.wait_recv()

    def exchange(src, dst, number, tiles):
        def one(step, carry):
            other = lax.rem(ctx + step, N_CTX)
            pltpu.make_async_remote_copy(
                src_ref=src.at[pl.ds(other * tiles, tiles)],
                dst_ref=dst.at[pl.ds(ctx * tiles, tiles)],
                send_sem=scan_sem.at[0, number],
                recv_sem=scan_sem.at[1, number],
                device_id=(other, dp),
                device_id_type=MESH,
            ).start()
            return carry

        lax.fori_loop(1, N_CTX, one, 0)
        dst[pl.ds(ctx * tiles, tiles)] = src[pl.ds(ctx * tiles, tiles)]

    def exchanged(src, dst, number, tiles):
        most = pl.ds(0, (N_CTX - 1) * tiles)
        pltpu.make_async_copy(src.at[most], dst.at[most], scan_sem.at[1, number]).wait()
        pltpu.make_async_copy(src.at[most], dst.at[most], scan_sem.at[0, number]).wait()

    def prefix(inbox, outbox, tiles, reverse):
        def add(step, total):
            source = N_CTX - 1 - step if reverse else step
            outbox[pl.ds(source * tiles, tiles)] = total.astype(BF16)
            return total + inbox[pl.ds(source * tiles, tiles)].astype(F32)

        lax.fori_loop(0, N_CTX, add, jnp.zeros((tiles, 16, HEAD), F32))

    def columns(head):
        return pl.ds(pl.multiple_of(head * HEAD, HEAD), HEAD)

    def lower():
        rows = lax.broadcasted_iota(jnp.int32, (TOK, TOK), 0)
        return rows >= lax.broadcasted_iota(jnp.int32, (TOK, TOK), 1)

    def upper():
        rows = lax.broadcasted_iota(jnp.int32, (TOK, TOK), 0)
        return rows <= lax.broadcasted_iota(jnp.int32, (TOK, TOK), 1)

    def own_memory(head, carry):
        cols = columns(head)
        k = (keys[:, cols].astype(F32) * ksp[:, cols].astype(F32)).astype(BF16)
        keys[:, cols] = k
        state = dot(k, val[:, cols], TN).astype(BF16)
        m_send[pl.ds(head * 8, 8)] = state.reshape(8, 16, HEAD)
        return carry

    def own_query_grad(head, carry):
        cols = columns(head)
        grad_scores = jnp.where(lower(), dot(cot[:, cols], val[:, cols], NT), 0.0).astype(BF16)
        vgrad[:, cols] = dot(grad_scores, keys[:, cols])
        return carry

    def mask_grad(head, carry):
        cols = columns(head)
        state = m_state[pl.ds(head * 8, 8)].reshape(HEAD, HEAD)
        whole = vgrad[:, cols] + dot(cot[:, cols], state, NT)
        mg[:, cols] = (factor * whole * qsp[:, cols].astype(F32)).astype(BF16)
        return carry

    def attend(g):
        weight = wbuf[g].reshape(D, GCOLS)
        both = dot(tok[...], weight)
        for one in range(2):
            head = 2 * g + one
            cols = columns(head)
            q = both[:, one * HEAD : (one + 1) * HEAD] * qsp[:, cols].astype(F32)
            q = q.astype(BF16)
            k, v, c = keys[:, cols], val[:, cols], cot[:, cols]
            state = dot(q, c, TN).astype(BF16).reshape(8, 16, HEAD)
            if head < FIRST:
                a_send[pl.ds(head * 8, 8)] = state
            else:
                b_send[pl.ds((head - FIRST) * 8, 8)] = state
            scores = jnp.where(lower(), dot(q, k, NT), 0.0).astype(BF16)
            memory = m_state[pl.ds(head * 8, 8)].reshape(HEAD, HEAD)
            att[:, cols] = (factor * (dot(scores, v) + dot(q, memory))).astype(BF16)
            scores = jnp.where(upper(), dot(k, q, NT), 0.0).astype(BF16)
            vgrad[:, cols] = dot(scores, c)
            grad_scores = jnp.where(upper(), dot(v, c, NT), 0.0).astype(BF16)
            kgrad[:, cols] = dot(grad_scores, q)

    stores = []

    def token_grad(number, carry):
        low, y, pair = number // 8, lax.rem(number // 2, 4), lax.rem(number, 2)
        total = None
        for g in range(GROUPS):
            weight = wbuf[g, low, y, pl.ds(2 * pair, 2)].reshape(GCOLS, GCOLS)
            term = dot(mg[:, g * GCOLS : (g + 1) * GCOLS], weight, NT)
            total = term if total is None else total + term
        cols = pl.ds(pl.multiple_of(number * GCOLS, GCOLS), GCOLS)
        gtok[:, cols] = total.astype(BF16)
        return carry

    def finish(states, first_head):
        def one(head, carry):
            cols = columns(head)
            state = states[pl.ds((head - first_head) * 8, 8)].reshape(HEAD, HEAD)
            key_grad = kgrad[:, cols] + dot(val[:, cols], state, NT)
            gkey[:, cols] = (factor * key_grad * ksp[:, cols].astype(F32)).astype(BF16)
            value_grad = vgrad[:, cols] + dot(keys[:, cols], state)
            gval[:, cols] = (factor * value_grad).astype(BF16)
            return carry

        return one

    def store(src, dst, number):
        copy = pltpu.make_async_copy(src, dst, store_sem.at[number])
        copy.start()
        stores.append(copy)

    m_tiles, a_tiles, b_tiles = HEADS // 4, FIRST // 4, (HEADS - FIRST) // 4
    for g in range(GROUPS):
        first(g)
    for number in range(3):
        loads[number].wait()
    lax.fori_loop(0, HEADS, own_memory, 0)
    exchange(m_send, m_in, 0, m_tiles)
    for step in range(GROUPS + 7):
        if step < GROUPS:
            second(step)
        if 0 <= step - 1 < GROUPS:
            third(step - 1)
        if 0 <= step - 4 < GROUPS:
            fourth(step - 4)
        if 0 <= step - 6 < GROUPS:
            fifth(step - 6)
        if step == 0:
            loads[3].wait()
        if step < 4:
            lax.fori_loop(4 * step, 4 * step + 4, own_query_grad, 0)
        if step == 3:
            exchanged(m_send, m_in, 0, m_tiles)
            prefix(m_in, m_out, m_tiles, False)
            exchange(m_out, m_state, 1, m_tiles)
        if step == 6:
            exchanged(m_out, m_state, 1, m_tiles)
            loads[4].wait()
            loads[5].wait()
            lax.fori_loop(0, HEADS, mask_grad, 0)
        if 0 <= step - 7 < GROUPS:
            arrived(step - 7)
            attend(step - 7)
        if 2 * (step - 6) == FIRST:
            exchange(a_send, a_in, 2, a_tiles)
        if 2 * (step - 7) == FIRST:
            exchanged(a_send, a_in, 2, a_tiles)
            prefix(a_in, a_out, a_tiles, True)
            exchange(a_out, a_state, 3, a_tiles)
    exchange(b_send, b_in, 4, b_tiles)
    store(att, att_hbm, 0)
    lax.fori_loop(0, 5, token_grad, 0)
    exchanged(b_send, b_in, 4, b_tiles)
    prefix(b_in, b_out, b_tiles, True)
    exchange(b_out, b_state, 5, b_tiles)
    lax.fori_loop(5, 16, token_grad, 0)
    store(gtok, gtok_hbm, 1)
    exchanged(a_out, a_state, 3, a_tiles)
    lax.fori_loop(0, FIRST, finish(a_state, 0), 0)
    exchanged(b_out, b_state, 5, b_tiles)
    lax.fori_loop(FIRST, HEADS, finish(b_state, FIRST), 0)
    store(gkey, gkey_hbm, 2)
    store(gval, gval_hbm, 3)
    for copy in ended:
        copy.wait_send()
    for copy in stores:
        copy.wait()


def scan_buffers(heads):
    return [pltpu.VMEM((heads * 8, 16, HEAD), BF16)] * 4


def layer(factor, tokens, key_input, values, q_weight, q_spikes, k_spikes, cotangent):
    wide = pltpu.VMEM((TOK, HD), BF16)
    wide_float = pltpu.VMEM((TOK, HD), F32)
    wide_int = pltpu.VMEM((TOK, HD), jnp.int32)
    anywhere = pl.BlockSpec(memory_space=pl.ANY)
    narrow = jax.ShapeDtypeStruct((TOK, HD), BF16)
    return pl.pallas_call(
        functools.partial(layer_kernel, factor),
        out_shape=(narrow, jax.ShapeDtypeStruct((TOK, D), BF16), narrow, narrow),
        in_specs=[anywhere] * 7,
        out_specs=(anywhere,) * 4,
        scratch_shapes=[
            pltpu.VMEM((GROUPS, 2, 4, 4, 2, 2, ROWS, GCOLS), BF16),
            pltpu.VMEM((TOK, D), BF16),
            wide,
            wide,
            wide,
            wide_int,
            wide_int,
            wide,
            wide_float,
            wide_float,
            wide,
            pltpu.VMEM((TOK, D), BF16),
            wide,
            wide,
            *scan_buffers(HEADS),
            *scan_buffers(FIRST),
            *scan_buffers(HEADS - FIRST),
            pltpu.SemaphoreType.DMA((GROUPS,)),
            pltpu.SemaphoreType.DMA((6,)),
            pltpu.SemaphoreType.DMA((GROUPS, 10)),
            pltpu.SemaphoreType.DMA((GROUPS, 10)),
            pltpu.SemaphoreType.DMA((2, GROUPS, 4)),
            pltpu.SemaphoreType.DMA((2, 6)),
            pltpu.SemaphoreType.DMA((4,)),
        ],
        compiler_params=pltpu.CompilerParams(
            collective_id=0, has_side_effects=True, vmem_limit_bytes=60 << 20
        ),
    )(tokens, key_input, values, q_weight, q_spikes, k_spikes, cotangent)


def per_device(tokens, key_input, values, q_weight, q_spikes, k_spikes, cotangent):
    sequence = tokens.shape[1] * lax.axis_size("ctx")
    factor = 3.0 / math.sqrt(HEAD * sequence)
    outs = layer(
        factor, tokens[0], key_input[0], values[0], q_weight, q_spikes[0], k_spikes[0], cotangent[0]
    )
    return tuple(out[None] for out in outs)


def solution(mesh):
    rows = P("dp", "ctx", None)
    in_specs = (rows, rows, rows, P(("ctx", "dp"), None), rows, rows, rows)
    return jax.shard_map(
        per_device, mesh=mesh, in_specs=in_specs, out_specs=(rows,) * 4, check_vma=False
    )
```

time: 1040 us -> 122 us (0.12)
  waiting for transfers between devices: 870 us -> 0 us
  Pallas kernels: 0 us -> 113 us
  matrix products: 73 us -> 0 us
  other arithmetic: 52.8 us -> 0 us
  local copies, waits for them, and re-layouts: 25.8 us -> 8.54 us
  between operations: 13.9 us -> 0.65 us
    all_gather x3 -> x0, waiting for transfers between devices: 869 us -> none  [the longest x2 665 us: entering(): gathered = lax.all_gather(part, axis)]
    pallas_call x0 -> x1, Pallas kernels: none -> 113 us  [layer(): pl.pallas_call(functools.partial(layer_kernel, factor), out_shape=(narrow...]
    dot_general x14 -> x0, matrix products: 73 us -> none  [the longest x1 13.4 us: per_device(): lax.dot_general(masked_rows, lax.all_gather(q_weight, ('ctx', 'dp'), axis...]
    add x31 -> x0, other arithmetic: 46.2 us -> none  [add_states(): return first_part + second_part]
  transfers between devices with their start and end apart: 3 -> 0, of which waited for: 3 -> 0; matrix products, arithmetic and copies ran while one was open for 7% -> 0% of each run, Pallas kernels for 0% -> 0%
where the time goes in v2:
time: 122 us
  Pallas kernels  113 us (93%)
  local copies, waits for them, and re-layouts  8.54 us (7%)
    pallas_call x1, Pallas kernels, layer(): pl.pallas_call(functools.partial(layer_kernel, factor), out_shape=(narrow...  113 us
    unnamed x10, local copies, waits for them, and re-layouts  8.54 us

profile of v2, /device:TPU:0, one launch (start us, length us, event | category | flops | bytes accessed | tf_op | source)
XLA Modules:
  0.0 122.3 jit_solution(14059894239729839734)
XLA Ops:
  0.6 113.1 %shard_map.102 = (bf16[384,2048]{1,0:T(8,128)(2,1)}, bf16[384,4096]{1,0:T(8,128)(2,1)}, bf16[384,2048]{1,0:T(8,128)(2,1)}, bf16[384,2048]{1,0:T(8,128)(2,1)}) custom-call(bf16[384,4096]{1,0:T(8,128)(2,1)} %bitcast.10, bf16[384,2048]{1,0:T(8,128)(2,1)} %bitcast.14, bf16[384,2048]{1,0:T(8,128)(2,1)} %bitcast.15, bf16[32,2048]{1,0:T(8,128)(2,1)} %w_hbm.1, ...), custom_call_target="tpu_custom_call" | custom-call | tf_op jit(solution)/shard_map/pallas_call | solution.py:427
  113.7 0.0 copy-start
  113.7 2.9 %copy.15 = bf16[1,384,2048]{2,1,0:T(8,128)(2,1)} copy(bf16[1,384,2048]{2,1,0:T(8,128)(2,1)} %bitcast.19) | data formatting | bytes 3145728
  116.6 0.0 copy-done
  116.6 0.0 copy-start.2
  116.6 1.7 %copy.16 = bf16[1,384,4096]{2,1,0:T(8,128)(2,1)} copy(bf16[1,384,4096]{2,1,0:T(8,128)(2,1)S(1)} %bitcast.13) | data formatting | bytes 6291456
  118.3 0.9 copy-done.2
  119.2 0.0 copy-start.1
  119.2 1.1 copy.17
  120.3 0.8 copy-done.1
  121.2 1.1 copy.18
Async XLA Ops:
  113.7 2.9 %copy-start = (bf16[384,4096]{1,0:T(8,128)(2,1)S(1)}, bf16[384,4096]{1,0:T(8,128)(2,1)}, u32[]{:S(2)}) copy-start(bf16[384,4096]{1,0:T(8,128)(2,1)} %get-tuple-element.9) | copy-start | bytes 9437188
  116.6 2.5 %copy-start.2 = (bf16[384,2048]{1,0:T(8,128)(2,1)S(1)}, bf16[384,2048]{1,0:T(8,128)(2,1)}, u32[]{:S(2)}) copy-start(bf16[384,2048]{1,0:T(8,128)(2,1)} %get-tuple-element.10) | copy-start | bytes 4718596
  119.2 2.0 %copy-start.1 = (bf16[384,2048]{1,0:T(8,128)(2,1)S(1)}, bf16[384,2048]{1,0:T(8,128)(2,1)}, u32[]{:S(2)}) copy-start(bf16[384,2048]{1,0:T(8,128)(2,1)} %get-tuple-element.11) | copy-start | bytes 4718596

commit v3 on v2

v3 whole, which is shorter than its diff:
```python
import functools
import math

import jax
import jax.numpy as jnp
from jax import lax
from jax.experimental import pallas as pl
from jax.experimental.pallas import tpu as pltpu
from jax.sharding import PartitionSpec as P

HEADS = 16
HEAD = 128
TOK = 384
D = 4096
HD = HEADS * HEAD
GROUPS = 8
GCOLS = 256
N_CTX = 32
ROWS = 32
FIRST = 12
CHUNK = 512
AHEAD = 3
LAGS = (0, 3, 5, 6)
MESH = pl.DeviceIdType.MESH
ORDERS = ((0, 1, 2), (1, 2, 0), (2, 0, 1))
BF16 = jnp.bfloat16
F32 = jnp.float32
NT = (((1,), (1,)), ((), ()))
TN = (((0,), (0,)), ((), ()))


def place():
    ctx = lax.axis_index("ctx")
    dp = lax.axis_index("dp")
    x = lax.rem(ctx, 4)
    y = lax.rem(ctx // 4, 4)
    z = (dp // 2) * 2 + ctx // 16
    return (x, y, z), lax.rem(dp, 2)


def device_of(at, core):
    x, y, z = at
    return (lax.rem(z, 2) * 16 + y * 4 + x, (z // 2) * 2 + core)


def moved(at, axis, by):
    out = list(at)
    out[axis] = lax.rem(out[axis] + by, 4)
    return tuple(out)


def view(buf, group, at, core, whole, half=None):
    picks = []
    for axis in range(2):
        if half is not None and half[0] == axis:
            picks.append(pl.ds(2 * half[1], 2))
        elif axis in whole:
            picks.append(slice(None))
        else:
            picks.append(at[axis])
    low = slice(None) if 2 in whole else lax.rem(at[2], 2)
    high = slice(None) if 2 in whole else at[2] // 2
    return buf.at[group, low, picks[1], picks[0], high, core]


def dot(a, b, dims=(((1,), (0,)), ((), ()))):
    return lax.dot_general(a, b, dims, preferred_element_type=F32)


def layer_kernel(
    factor,
    tok_hbm,
    key_hbm,
    val_hbm,
    w_hbm,
    qsp_hbm,
    ksp_hbm,
    cot_hbm,
    att,
    gtok,
    gkey,
    gval,
    wbuf,
    tok,
    keys,
    val,
    cot,
    qsp,
    ksp,
    mg,
    kgrad,
    vgrad,
    qgrad,
    projected,
    queries,
    local,
    m_send,
    m_in,
    m_out,
    m_state,
    a_send,
    a_in,
    a_out,
    a_state,
    own_sem,
    load_sem,
    send_sem,
    recv_sem,
    sib_sem,
    scan_sem,
):
    at, core = place()
    ctx = lax.axis_index("ctx")
    dp = lax.axis_index("dp")
    other_core = device_of(at, 1 - core)

    own = []
    for g in range(GROUPS):
        copy = pltpu.make_async_copy(
            w_hbm.at[:, pl.ds(g * GCOLS, GCOLS)], view(wbuf, g, at, core, ()), own_sem.at[g]
        )
        copy.start()
        own.append(copy)

    loads = []
    for number, (src, dst) in enumerate(
        (
            (key_hbm, keys),
            (ksp_hbm, ksp),
            (val_hbm, val),
            (cot_hbm, cot),
            (tok_hbm, tok),
            (qsp_hbm, qsp),
        )
    ):
        copy = pltpu.make_async_copy(src, dst, load_sem.at[number])
        copy.start()
        loads.append(copy)

    barrier = pltpu.get_barrier_semaphore()

    def greet(step, carry):
        pl.semaphore_signal(
            barrier, 1, device_id=(lax.rem(ctx + step, N_CTX), dp), device_id_type=MESH
        )
        return carry

    lax.fori_loop(1, N_CTX, greet, 0)
    far_z = 1 - at[2] // 2
    for low in (0, 1):
        pl.semaphore_signal(
            barrier,
            1,
            device_id=(low * 16 + at[1] * 4 + at[0], far_z * 2 + core),
            device_id_type=MESH,
        )
    pl.semaphore_signal(barrier, 1, device_id=other_core, device_id_type=MESH)
    pl.semaphore_wait(barrier, N_CTX + 2)

    def remote(part, sems, target):
        return pltpu.make_async_remote_copy(
            src_ref=part,
            dst_ref=part,
            send_sem=sems[0],
            recv_sem=sems[1],
            device_id=target,
            device_id_type=MESH,
        )

    def link(part, g, slot, target):
        return remote(part, (send_sem.at[g, slot], recv_sem.at[g, slot]), target)

    def spread(g, order, number):
        part = view(wbuf, g, at, core, order[:number])
        return [
            link(part, g, 3 * number + by - 1, device_of(moved(at, order[number], by), core))
            for by in (1, 3, 2)
        ]

    def near(g, order):
        part = view(wbuf, g, at, core, order[:2])
        return [
            link(part, g, 5 + way, device_of(moved(at, order[2], by), core))
            for way, by in ((1, 1), (2, 3))
        ]

    def far(g, order):
        left, right = moved(at, order[2], 3), moved(at, order[2], 1)
        split = 0 if order[2] == 1 else 1
        return [
            link(view(wbuf, g, here, core, order[:2], (split, half)), g, 8 + half, device_of(to, core))
            for half, here, to in ((0, left, right), (1, right, left))
        ]

    def sibling(g, order):
        return [
            remote(
                view(wbuf, g, moved(at, order[2], by), core, order[:2]),
                (sib_sem.at[0, g, by], sib_sem.at[1, g, by]),
                other_core,
            )
            for by in range(4)
        ]

    def ordered(g, act):
        for number, order in enumerate(ORDERS):

            @pl.when(lax.rem(g + core, 3) == number)
            def _(order=order):
                act(g, order)

    def start(copies):
        for copy in copies:
            copy.start()

    def first(g, order):
        start(spread(g, order, 0))

    def second(g, order):
        for copy in spread(g, order, 0):
            copy.wait_recv()
        start(spread(g, order, 1))

    def third(g, order):
        for copy in spread(g, order, 1):
            copy.wait_recv()
        start(near(g, order))
        sibling(g, order)[0].start()

    def fourth(g, order):
        arriving, onward, across = near(g, order), far(g, order), sibling(g, order)
        for half, by in ((0, 3), (1, 1)):
            arriving[half].wait_recv()
            onward[half].start()
            across[by].start()

    def fifth(g, order):
        for copy in far(g, order):
            copy.wait_recv()
        sibling(g, order)[2].start()

    def arrived(g, order):
        for copy in sibling(g, order):
            copy.wait_recv()

    def sent(g, order):
        for copy in (
            *spread(g, order, 0),
            *spread(g, order, 1),
            *near(g, order),
            *far(g, order),
            *sibling(g, order),
        ):
            copy.wait_send()

    def exchange(src, dst, number, tiles, base=0):
        def one(step, carry):
            other = lax.rem(ctx + step, N_CTX)
            pltpu.make_async_remote_copy(
                src_ref=src.at[pl.ds(base + other * tiles, tiles)],
                dst_ref=dst.at[pl.ds(base + ctx * tiles, tiles)],
                send_sem=scan_sem.at[0, number],
                recv_sem=scan_sem.at[1, number],
                device_id=(other, dp),
                device_id_type=MESH,
            ).start()
            return carry

        lax.fori_loop(1, N_CTX, one, 0)
        mine = pl.ds(base + ctx * tiles, tiles)
        dst[mine] = src[mine]

    def exchanged(src, dst, number, tiles, base=0):
        most = pl.ds(base, (N_CTX - 1) * tiles)
        pltpu.make_async_copy(src.at[most], dst.at[most], scan_sem.at[1, number]).wait()
        pltpu.make_async_copy(src.at[most], dst.at[most], scan_sem.at[0, number]).wait()

    def prefix(inbox, outbox, tiles, reverse, base=0):
        def add(step, total):
            source = N_CTX - 1 - step if reverse else step
            piece = pl.ds(base + source * tiles, tiles)
            outbox[piece] = total.astype(BF16)
            return total + inbox[piece].astype(F32)

        lax.fori_loop(0, N_CTX, add, jnp.zeros((tiles, 16, HEAD), F32))

    def columns(head):
        return pl.ds(pl.multiple_of(head * HEAD, HEAD), HEAD)

    def keep(product, first_row, first_col, below):
        rows = lax.broadcasted_iota(jnp.int32, product.shape, 0) + first_row
        cols = lax.broadcasted_iota(jnp.int32, product.shape, 1) + first_col
        return jnp.where(rows >= cols if below else rows <= cols, product, 0.0).astype(BF16)

    def below(a, b, c):
        wide = dot(keep(dot(a, b[:256], NT), 0, 0, True), c[:256])
        last = dot(keep(dot(a[256:], b[256:], NT), 0, 0, True), c[256:])
        return jnp.concatenate([wide[:256], wide[256:] + last], axis=0)

    def above(a, b, c):
        wide = dot(keep(dot(a, b[128:], NT), 0, 128, False), c[128:])
        head = dot(keep(dot(a[:128], b[:128], NT), 0, 0, False), c[:128])
        return jnp.concatenate([wide[:128] + head, wide[128:]], axis=0)

    def own_memory(head, carry):
        cols = columns(head)
        k = (keys[:, cols].astype(F32) * ksp[:, cols].astype(F32)).astype(BF16)
        keys[:, cols] = k
        state = dot(k, val[:, cols], TN).astype(BF16)
        m_send[pl.ds(head * 8, 8)] = state.reshape(8, 16, HEAD)
        return carry

    def own_query_grad(head, carry):
        cols = columns(head)
        qgrad[:, cols] = below(cot[:, cols], val[:, cols], keys[:, cols])
        return carry

    def use_memory(head, carry):
        cols = columns(head)
        state = m_state[pl.ds(head * 8, 8)].reshape(HEAD, HEAD)
        whole = qgrad[:, cols] + dot(cot[:, cols], state, NT)
        mg[:, cols] = (factor * whole * qsp[:, cols].astype(F32)).astype(BF16)
        att[:, cols] = (factor * (local[:, cols] + dot(queries[:, cols], state))).astype(BF16)
        return carry

    def project(g):
        projected[...] = dot(tok[...], wbuf[g].reshape(D, GCOLS))

    def attend(g):
        for one in range(2):
            head = 2 * g + one
            cols = columns(head)
            q = projected[:, one * HEAD : (one + 1) * HEAD] * qsp[:, cols].astype(F32)
            q = q.astype(BF16)
            queries[:, cols] = q
            k, v, c = keys[:, cols], val[:, cols], cot[:, cols]
            state = dot(q, c, TN).astype(BF16).reshape(8, 16, HEAD)
            a_send[pl.ds(head * 8, 8)] = state
            local[:, cols] = below(q, k, v)
            vgrad[:, cols] = above(k, q, c)
            kgrad[:, cols] = above(v, c, q)

    def token_grad(number, carry):
        pieces = [
            wbuf[g, number // 4, lax.rem(number, 4)].reshape(CHUNK, GCOLS) for g in range(GROUPS)
        ]
        total = dot(mg[...], jnp.concatenate(pieces, axis=1), NT)
        cols = pl.ds(pl.multiple_of(number * CHUNK, CHUNK), CHUNK)
        gtok[:, cols] = total.astype(BF16)
        return carry

    def finish(head, carry):
        cols = columns(head)
        state = a_state[pl.ds(head * 8, 8)].reshape(HEAD, HEAD)
        key_grad = kgrad[:, cols] + dot(val[:, cols], state, NT)
        gkey[:, cols] = (factor * key_grad * ksp[:, cols].astype(F32)).astype(BF16)
        value_grad = vgrad[:, cols] + dot(keys[:, cols], state)
        gval[:, cols] = (factor * value_grad).astype(BF16)
        return carry

    m_tiles, a_tiles, b_tiles = HEADS // 4, FIRST // 4, (HEADS - FIRST) // 4
    b_base = FIRST * 8
    for copy in own:
        copy.wait()

    def begin(g, carry):
        ordered(g, first)
        return carry

    lax.fori_loop(0, GROUPS, begin, 0)
    for number in range(4):
        loads[number].wait()
    lax.fori_loop(0, HEADS, own_memory, 0, unroll=2)

    def ahead(g, carry):
        ordered(g, second)
        return carry

    lax.fori_loop(0, AHEAD, ahead, 0)
    exchange(m_send, m_in, 0, m_tiles)

    def body(step, carry):
        for lag, act in zip((-AHEAD, *LAGS), (second, third, fourth, fifth, arrived)):
            low = max(lag, 0)

            @pl.when((step >= low) & (step < lag + GROUPS))
            def _(lag=lag, act=act):
                ordered(step - lag, act)

        last = LAGS[3]

        @pl.when(step < 4)
        def _():
            for pair in range(2):
                for one in range(2):
                    own_query_grad(4 * step + 2 * pair + one, 0)

        @pl.when(step == 5)
        def _():
            exchanged(m_send, m_in, 0, m_tiles)
            prefix(m_in, m_out, m_tiles, False)
            exchange(m_out, m_state, 1, m_tiles)

        @pl.when(step == last)
        def _():
            loads[4].wait()
            loads[5].wait()

        @pl.when(step >= last)
        def _():
            project(step - last)

        @pl.when((step >= last) & (step >= 0))
        def _():
            attend(step - last)

        @pl.when(2 * (step - last + 1) == FIRST)
        def _():
            exchange(a_send, a_in, 2, a_tiles)

        return carry

    lax.fori_loop(0, GROUPS + LAGS[3], body, 0)
    exchange(a_send, a_in, 4, b_tiles, b_base)
    exchanged(a_send, a_in, 2, a_tiles)
    prefix(a_in, a_out, a_tiles, True)
    exchange(a_out, a_state, 3, a_tiles)
    exchanged(m_out, m_state, 1, m_tiles)
    lax.fori_loop(0, HEADS, use_memory, 0, unroll=2)
    exchanged(a_send, a_in, 4, b_tiles, b_base)
    prefix(a_in, a_out, b_tiles, True, b_base)
    exchange(a_out, a_state, 5, b_tiles, b_base)
    lax.fori_loop(0, 8, token_grad, 0)
    exchanged(a_out, a_state, 3, a_tiles)
    lax.fori_loop(0, FIRST, finish, 0, unroll=2)
    exchanged(a_out, a_state, 5, b_tiles, b_base)
    lax.fori_loop(FIRST, HEADS, finish, 0, unroll=2)

    def end(g, carry):
        ordered(g, sent)
        return carry

    lax.fori_loop(0, GROUPS, end, 0)


def scan_buffers(heads):
    return [pltpu.VMEM((heads * 8, 16, HEAD), BF16)] * 4


def layer(factor, tokens, key_input, values, q_weight, q_spikes, k_spikes, cotangent):
    wide = pltpu.VMEM((TOK, HD), BF16)
    wide_float = pltpu.VMEM((TOK, HD), F32)
    wide_int = pltpu.VMEM((TOK, HD), jnp.int32)
    anywhere = pl.BlockSpec(memory_space=pl.ANY)
    return pl.pallas_call(
        functools.partial(layer_kernel, factor),
        out_shape=(wide, pltpu.VMEM((TOK, D), BF16), wide, wide),
        in_specs=[anywhere] * 7,
        out_specs=(pl.BlockSpec(memory_space=pltpu.VMEM),) * 4,
        scratch_shapes=[
            pltpu.VMEM((GROUPS, 2, 4, 4, 2, 2, ROWS, GCOLS), BF16),
            pltpu.VMEM((TOK, D), BF16),
            wide,
            wide,
            wide,
            wide_int,
            wide_int,
            wide,
            wide_float,
            wide_float,
            wide_float,
            pltpu.VMEM((TOK, GCOLS), F32),
            wide,
            wide_float,
            *scan_buffers(HEADS),
            *scan_buffers(HEADS),
            pltpu.SemaphoreType.DMA((GROUPS,)),
            pltpu.SemaphoreType.DMA((6,)),
            pltpu.SemaphoreType.DMA((GROUPS, 10)),
            pltpu.SemaphoreType.DMA((GROUPS, 10)),
            pltpu.SemaphoreType.DMA((2, GROUPS, 4)),
            pltpu.SemaphoreType.DMA((2, 6)),
        ],
        compiler_params=pltpu.CompilerParams(
            collective_id=0, has_side_effects=True, vmem_limit_bytes=54 << 20
        ),
    )(tokens, key_input, values, q_weight, q_spikes, k_spikes, cotangent)


def per_device(tokens, key_input, values, q_weight, q_spikes, k_spikes, cotangent):
    sequence = tokens.shape[1] * lax.axis_size("ctx")
    factor = 3.0 / math.sqrt(HEAD * sequence)
    outs = layer(
        factor, tokens[0], key_input[0], values[0], q_weight, q_spikes[0], k_spikes[0], cotangent[0]
    )
    return tuple(out[None] for out in outs)


def solution(mesh):
    rows = P("dp", "ctx", None)
    in_specs = (rows, rows, rows, P(("ctx", "dp"), None), rows, rows, rows)
    return jax.shard_map(
        per_device, mesh=mesh, in_specs=in_specs, out_specs=(rows,) * 4, check_vma=False
    )
```

time: 122 us -> 93.3 us (0.76)
  Pallas kernels: 113 us -> 87.4 us
  local copies, waits for them, and re-layouts: 8.54 us -> 5.09 us
    pallas_call x1, Pallas kernels: 113 us -> 87.4 us  [layer(): pl.pallas_call(functools.partial(layer_kernel, factor), out_shape=(wide,...]
    unnamed x10 -> x4, local copies, waits for them, and re-layouts: 8.54 us -> 5.09 us
where the time goes in v3:
time: 93.3 us; the launch traced here: 93.2 us
  Pallas kernels  87.4 us (94%)
  local copies, waits for them, and re-layouts  5.09 us (5%)
    pallas_call x1, Pallas kernels, layer(): pl.pallas_call(functools.partial(layer_kernel, factor), out_shape=(wide,...  87.4 us
    unnamed x4, local copies, waits for them, and re-layouts  5.09 us

profile of v3, /device:TPU:0, one launch (start us, length us, event | category | flops | bytes accessed | tf_op | source)
XLA Modules:
  0.0 93.2 jit_solution(7602435829687047585)
XLA Ops:
  0.6 87.4 %shard_map.102 = (bf16[384,2048]{1,0:T(8,128)(2,1)S(1)}, bf16[384,4096]{1,0:T(8,128)(2,1)S(1)}, bf16[384,2048]{1,0:T(8,128)(2,1)S(1)}, bf16[384,2048]{1,0:T(8,128)(2,1)S(1)}) custom-call(bf16[384,4096]{1,0:T(8,128)(2,1)} %bitcast.14, bf16[384,2048]{1,0:T(8,128)(2,1)} %bitcast.17, bf16[384,2048]{1,0:T(8,128)(2,1)} %bitcast.18, bf16[32,2048]{1,0:T(8,128)(2,1)} %w_hbm.1, ...), custom_call_target="tpu_custom_call" | custom-call | tf_op jit(solution)/shard_map/pallas_call | solution.py:455
  88.1 1.1 %copy.15 = bf16[1,384,2048]{2,1,0:T(8,128)(2,1)} copy(bf16[1,384,2048]{2,1,0:T(8,128)(2,1)S(1)} %bitcast.13) | data formatting | bytes 3145728
  89.2 1.7 %copy.16 = bf16[1,384,4096]{2,1,0:T(8,128)(2,1)} copy(bf16[1,384,4096]{2,1,0:T(8,128)(2,1)S(1)} %bitcast.10) | data formatting | bytes 6291456
  90.9 1.1 %copy.17 = bf16[1,384,2048]{2,1,0:T(8,128)(2,1)} copy(bf16[1,384,2048]{2,1,0:T(8,128)(2,1)S(1)} %bitcast.12) | data formatting | bytes 3145728
  92.0 1.1 %copy.18 = bf16[1,384,2048]{2,1,0:T(8,128)(2,1)} copy(bf16[1,384,2048]{2,1,0:T(8,128)(2,1)S(1)} %bitcast.11) | data formatting | bytes 3145728

commit v4 on v3

--- a/solution.py
+++ b/solution.py
@@ -21,6 +21,8 @@
 CHUNK = 512
 AHEAD = 3
 LAGS = (0, 3, 5, 6)
+MEMORY_STEP = 9
+QUERY_STEP = 2
 MESH = pl.DeviceIdType.MESH
 ORDERS = ((0, 1, 2), (1, 2, 0), (2, 0, 1))
 BF16 = jnp.bfloat16
@@ -368,15 +370,15 @@
         return carry
 
     lax.fori_loop(0, GROUPS, begin, 0)
+
+    def ahead(g, carry):
+        ordered(g, second)
+        return carry
+
+    lax.fori_loop(0, AHEAD, ahead, 0)
     for number in range(4):
         loads[number].wait()
     lax.fori_loop(0, HEADS, own_memory, 0, unroll=2)
-
-    def ahead(g, carry):
-        ordered(g, second)
-        return carry
-
-    lax.fori_loop(0, AHEAD, ahead, 0)
     exchange(m_send, m_in, 0, m_tiles)
 
     def body(step, carry):
@@ -389,13 +391,13 @@
 
         last = LAGS[3]
 
-        @pl.when(step < 4)
+        @pl.when((step >= QUERY_STEP) & (step < QUERY_STEP + 4))
         def _():
             for pair in range(2):
                 for one in range(2):
-                    own_query_grad(4 * step + 2 * pair + one, 0)
-
-        @pl.when(step == 5)
+                    own_query_grad(4 * (step - QUERY_STEP) + 2 * pair + one, 0)
+
+        @pl.when(step == MEMORY_STEP)
         def _():
             exchanged(m_send, m_in, 0, m_tiles)
             prefix(m_in, m_out, m_tiles, False)
@@ -487,13 +489,36 @@
     )(tokens, key_input, values, q_weight, q_spikes, k_spikes, cotangent)
 
 
+def write_kernel(*refs):
+    sources, targets, sems = refs[:4], refs[4:8], refs[8]
+    copies = [
+        pltpu.make_async_copy(src, dst, sems.at[number])
+        for number, (src, dst) in enumerate(zip(sources, targets))
+    ]
+    for copy in copies:
+        copy.start()
+    for copy in copies:
+        copy.wait()
+
+
+def write(arrays):
+    return pl.pallas_call(
+        write_kernel,
+        out_shape=[jax.ShapeDtypeStruct(array.shape, array.dtype) for array in arrays],
+        in_specs=[pl.BlockSpec(memory_space=pltpu.VMEM)] * 4,
+        out_specs=[pl.BlockSpec(memory_space=pl.ANY)] * 4,
+        scratch_shapes=[pltpu.SemaphoreType.DMA((4,))],
+        compiler_params=pltpu.CompilerParams(vmem_limit_bytes=1 << 20),
+    )(*arrays)
+
+
 def per_device(tokens, key_input, values, q_weight, q_spikes, k_spikes, cotangent):
     sequence = tokens.shape[1] * lax.axis_size("ctx")
     factor = 3.0 / math.sqrt(HEAD * sequence)
     outs = layer(
         factor, tokens[0], key_input[0], values[0], q_weight, q_spikes[0], k_spikes[0], cotangent[0]
     )
-    return tuple(out[None] for out in outs)
+    return tuple(out[None] for out in write(outs))
 
 
 def solution(mesh):

time: 93.3 us -> 90.2 us (0.967)
  local copies, waits for them, and re-layouts: 5.09 us -> 0 us
  Pallas kernels: 87.4 us -> 89.5 us
    unnamed x4 -> x0, local copies, waits for them, and re-layouts: 5.09 us -> none
    pallas_call x0 -> x1, Pallas kernels: none -> 3.21 us  [write(): pl.pallas_call(write_kernel, out_shape=[jax.ShapeDtypeStruct(array.shape,...]
    pallas_call x1, Pallas kernels: 87.4 us -> 86.3 us  [layer(): pl.pallas_call(functools.partial(layer_kernel, factor), out_shape=(wide,...]
where the time goes in v4:
time: 90.2 us; the launch traced here: 90.1 us
  Pallas kernels  89.5 us (99%)
    pallas_call x1, Pallas kernels, layer(): pl.pallas_call(functools.partial(layer_kernel, factor), out_shape=(wide,...  86.3 us
    pallas_call x1, Pallas kernels, write(): pl.pallas_call(write_kernel, out_shape=[jax.ShapeDtypeStruct(array.shape,...  3.21 us

profile of v4, /device:TPU:0, one launch (start us, length us, event | category | flops | bytes accessed | tf_op | source)
XLA Modules:
  0.0 90.1 jit_solution(10347070724104161752)
XLA Ops:
  0.6 86.3 %shard_map.102 = (bf16[384,2048]{1,0:T(8,128)(2,1)S(1)}, bf16[384,4096]{1,0:T(8,128)(2,1)S(1)}, bf16[384,2048]{1,0:T(8,128)(2,1)S(1)}, bf16[384,2048]{1,0:T(8,128)(2,1)S(1)}) custom-call(bf16[384,4096]{1,0:T(8,128)(2,1)} %bitcast.10, bf16[384,2048]{1,0:T(8,128)(2,1)} %bitcast.13, bf16[384,2048]{1,0:T(8,128)(2,1)} %bitcast.14, bf16[32,2048]{1,0:T(8,128)(2,1)} %w_hbm.1, ...), custom_call_target="tpu_custom_call" | custom-call | tf_op jit(solution)/shard_map/pallas_call | solution.py:457
  86.9 3.2 %shard_map.103 = (bf16[384,2048]{1,0:T(8,128)(2,1)}, bf16[384,4096]{1,0:T(8,128)(2,1)}, bf16[384,2048]{1,0:T(8,128)(2,1)}, bf16[384,2048]{1,0:T(8,128)(2,1)}) custom-call(bf16[384,2048]{1,0:T(8,128)(2,1)S(1)} %get-tuple-element.12.refs_0_, bf16[384,4096]{1,0:T(8,128)(2,1)S(1)} %get-tuple-element.13.refs_1_, bf16[384,2048]{1,0:T(8,128)(2,1)S(1)} %get-tuple-element.14.refs_2_, ...), custom_call_target="tpu_custom_call" | custom-call | tf_op jit(solution)/shard_map/pallas_call | solution.py:505

commit v5 on v4

--- a/solution.py
+++ b/solution.py
@@ -19,6 +19,7 @@
 ROWS = 32
 FIRST = 12
 CHUNK = 512
+STRIP = 96
 AHEAD = 3
 LAGS = (0, 3, 5, 6)
 MEMORY_STEP = 9
@@ -135,9 +136,9 @@
             (qsp_hbm, qsp),
         )
     ):
-        copy = pltpu.make_async_copy(src, dst, load_sem.at[number])
+        loads.append(pltpu.make_async_copy(src, dst, load_sem.at[number]))
+    for copy in loads[:3]:
         copy.start()
-        loads.append(copy)
 
     barrier = pltpu.get_barrier_semaphore()
 
@@ -376,10 +377,13 @@
         return carry
 
     lax.fori_loop(0, AHEAD, ahead, 0)
-    for number in range(4):
-        loads[number].wait()
+    for copy in loads[:3]:
+        copy.wait()
+    for copy in loads[3:]:
+        copy.start()
     lax.fori_loop(0, HEADS, own_memory, 0, unroll=2)
     exchange(m_send, m_in, 0, m_tiles)
+    loads[3].wait()
 
     def body(step, carry):
         for lag, act in zip((-AHEAD, *LAGS), (second, third, fourth, fifth, arrived)):
@@ -492,8 +496,11 @@
 def write_kernel(*refs):
     sources, targets, sems = refs[:4], refs[4:8], refs[8]
     copies = [
-        pltpu.make_async_copy(src, dst, sems.at[number])
+        pltpu.make_async_copy(
+            src.at[pl.ds(part * STRIP, STRIP)], dst.at[pl.ds(part * STRIP, STRIP)], sems.at[number, part]
+        )
         for number, (src, dst) in enumerate(zip(sources, targets))
+        for part in range(TOK // STRIP)
     ]
     for copy in copies:
         copy.start()
@@ -507,7 +514,7 @@
         out_shape=[jax.ShapeDtypeStruct(array.shape, array.dtype) for array in arrays],
         in_specs=[pl.BlockSpec(memory_space=pltpu.VMEM)] * 4,
         out_specs=[pl.BlockSpec(memory_space=pl.ANY)] * 4,
-        scratch_shapes=[pltpu.SemaphoreType.DMA((4,))],
+        scratch_shapes=[pltpu.SemaphoreType.DMA((4, TOK // STRIP))],
         compiler_params=pltpu.CompilerParams(vmem_limit_bytes=1 << 20),
     )(*arrays)
 

time: 90.2 us -> 90.2 us (level)
  no operation moved by 1% of the time
where the time goes in v5:
time: 90.2 us; the launch traced here: 89.9 us
  Pallas kernels  89.3 us (99%)
    pallas_call x1, Pallas kernels, layer(): pl.pallas_call(functools.partial(layer_kernel, factor), out_shape=(wide,...  86 us
    pallas_call x1, Pallas kernels, write(): pl.pallas_call(write_kernel, out_shape=[jax.ShapeDtypeStruct(array.shape,...  3.27 us

profile of v5, /device:TPU:0, one launch (start us, length us, event | category | flops | bytes accessed | tf_op | source)
XLA Modules:
  0.0 89.9 jit_solution(2975451466491409051)
XLA Ops:
  0.6 86.0 %shard_map.102 = (bf16[384,2048]{1,0:T(8,128)(2,1)S(1)}, bf16[384,4096]{1,0:T(8,128)(2,1)S(1)}, bf16[384,2048]{1,0:T(8,128)(2,1)S(1)}, bf16[384,2048]{1,0:T(8,128)(2,1)S(1)}) custom-call(bf16[384,4096]{1,0:T(8,128)(2,1)} %bitcast.10, bf16[384,2048]{1,0:T(8,128)(2,1)} %bitcast.13, bf16[384,2048]{1,0:T(8,128)(2,1)} %bitcast.14, bf16[32,2048]{1,0:T(8,128)(2,1)} %w_hbm.1, ...), custom_call_target="tpu_custom_call" | custom-call | tf_op jit(solution)/shard_map/pallas_call | solution.py:461
  86.6 3.3 %shard_map.103 = (bf16[384,2048]{1,0:T(8,128)(2,1)}, bf16[384,4096]{1,0:T(8,128)(2,1)}, bf16[384,2048]{1,0:T(8,128)(2,1)}, bf16[384,2048]{1,0:T(8,128)(2,1)}) custom-call(bf16[384,2048]{1,0:T(8,128)(2,1)S(1)} %get-tuple-element.12.refs_0_, bf16[384,4096]{1,0:T(8,128)(2,1)S(1)} %get-tuple-element.13.refs_1_, bf16[384,2048]{1,0:T(8,128)(2,1)S(1)} %get-tuple-element.14.refs_2_, ...), custom_call_target="tpu_custom_call" | custom-call | tf_op jit(solution)/shard_map/pallas_call | solution.py:512
